TPU v7x, 256 devices: a whole 4x4x8 slice. The times are simulated.
256 devices in a mesh: rep: 2 (over core), shard: 128 (over x, z, y).
Axes of the slice: x: 4, y: 4, z: 8, core: 2. Of those that a mesh axis runs over, the one named last changes fastest.
Arguments:
- grad: bfloat16 [192, 512, 2048], P(None, 'shard'), may hold values from -6 to 6
- momentum: bfloat16 [192, 512, 2048], P(None, 'shard'), may hold values from -6 to 6
- owners: int32 [2, 128, 2], replicated, may hold values from 0 to 192, as said below
Outputs:
- new_momentum: bfloat16 [192, 512, 2048], P(None, 'shard')
- update: bfloat16 [192, 512, 2048], P(None, 'shard')
Inputs may be any that keep to these rules, and one draw needn't show every extreme that they name: `owners`: no matrix index appears twice. In each device's row of 2 slots the entries naming matrices come before the empty ones (value 192). In every draw some device has all 2 slots filled, and some matrices are named by no slot.
All inputs are finite; a program needn't handle non-finite values.
Results may differ from a plain program's by a relative error of at most 0.013.
Values may be sent and summed in bfloat16 or wider, within the bound.
A program may use at most 128 MiB of HBM per device.

v0:
```python
import math
import jax
import jax.numpy as jnp
from jax import lax
from jax.sharding import PartitionSpec as P

R = 512
C = 2048
ITERS = 3
coef_a = 3.4445
coef_b = -4.775
coef_c = 2.0315
mom_decay = 0.95


def newton_schulz(matrix):
    whole = matrix.astype(jnp.float32)
    norm_value = jnp.sqrt(jnp.sum(whole * whole))
    current = (whole / (norm_value + 1e-07)).astype(jnp.bfloat16)
    scaled = None
    for turn_index in range(ITERS):
        gram = lax.dot_general(
            current, current, (((1,), (1,)), ((), ())), preferred_element_type=jnp.float32
        ).astype(jnp.bfloat16)
        square = jnp.dot(gram, gram, preferred_element_type=jnp.float32)
        mixer = (coef_b * gram.astype(jnp.float32) + coef_c * square).astype(jnp.bfloat16)
        result = coef_a * current.astype(jnp.float32) + jnp.dot(
            mixer, current, preferred_element_type=jnp.float32
        )
        if turn_index + 1 < ITERS:
            current = result.astype(jnp.bfloat16)
        else:
            scaled = (0.2 * math.sqrt(max(R, C)) * result).astype(jnp.bfloat16)
    return scaled


def spread_lists(owners, matrix_count, replicas, shard_count):
    devices = replicas * shard_count
    entries = owners.reshape(-1)
    alive = entries < matrix_count
    ordinal = jnp.cumsum(alive.astype(jnp.int32)) - 1
    per_device = (matrix_count + devices - 1) // devices
    target = jnp.where(alive, ordinal, devices * per_device)
    packed = (
        jnp.full((devices * per_device + 1,), matrix_count, jnp.int32)
        .at[target]
        .set(entries)[: devices * per_device]
    )
    return packed.reshape(per_device, shard_count, replicas).transpose(2, 1, 0)


def place_rows(returned, chosen, matrix_count):
    local_rows = returned.shape[1] // chosen.shape[1]
    pieces = returned.reshape(chosen.shape[0] * chosen.shape[1], local_rows, returned.shape[2])
    target = chosen.reshape(-1)
    empty = jnp.zeros((matrix_count, local_rows, returned.shape[2]), jnp.bfloat16)
    return empty.at[target].set(pieces, mode="drop")


def body(grad, momentum, owners):
    fresh = mom_decay * momentum.astype(jnp.float32) + grad.astype(jnp.float32)
    new_momentum = fresh.astype(jnp.bfloat16)
    nesterov = (grad.astype(jnp.float32) + mom_decay * fresh).astype(jnp.bfloat16)
    matrix_count = grad.shape[0]
    local_rows = grad.shape[1]
    width = grad.shape[2]
    replicas = lax.axis_size("rep")
    shard_count = lax.axis_size("shard")
    my_rep = lax.axis_index("rep")
    table = spread_lists(owners, matrix_count, replicas, shard_count)
    slot_count = table.shape[2]
    mine = lax.dynamic_index_in_dim(table, my_rep, 0, keepdims=False)
    chosen = mine.T
    usable = chosen < matrix_count
    taken = jnp.take(nesterov, jnp.minimum(chosen, matrix_count - 1), axis=0)
    outgoing = jnp.where(usable[:, :, None, None], taken, jnp.zeros_like(taken))
    outgoing = outgoing.reshape(slot_count, shard_count * local_rows, width)
    finished = lax.map(
        newton_schulz, lax.all_to_all(outgoing, "shard", split_axis=1, concat_axis=1, tiled=True)
    )
    returned = lax.all_to_all(finished, "shard", split_axis=1, concat_axis=1, tiled=True)
    both = lax.all_gather(returned, "rep", axis=0, tiled=True)
    every_choice = table.transpose(0, 2, 1).reshape(replicas * slot_count, shard_count)
    update = place_rows(both, every_choice, matrix_count)
    return (new_momentum, update)


def solution(mesh):
    placed = (P(None, "shard", None), P(None, "shard", None), P())
    return jax.shard_map(
        body,
        mesh=mesh,
        in_specs=placed,
        out_specs=(P(None, "shard", None), P(None, "shard", None)),
        check_vma=False,
    )
```

profile of v0, /device:TPU:1, one launch (start us, length us, event | category | flops | bytes accessed | tf_op | source)
XLA Modules:
  0.0 297.5 jit_solution(2510085038544679176)
XLA Ops:
  7.2 0.7 fusion.27
  7.9 0.8 copy.21
  10.1 2.4 scatter_custom_fusion
  13.1 7.1 %fusion = (bf16[192,4,2048]{2,1,0:T(4,128)(2,1)S(1)}, bf16[192,4,2048]{2,1,0:T(4,128)(2,1)}) fusion(bf16[192,4,2048]{2,1,0:T(4,128)(2,1)} %param.3, bf16[192,4,2048]{2,1,0:T(4,128)(2,1)} %param.4), kind=kLoop, calls=%fused_computation.5 | loop fusion | flops 12582912 | bytes 12582912 | tf_op jit(solution)/shard_map/convert_element_type | solution.py:63
  20.2 3.5 %gather_fusion = bf16[128,4,2048]{2,1,0:T(4,128)(2,1)} fusion(bf16[192,4,2048]{2,1,0:T(4,128)(2,1)S(1)} %get-tuple-element.15, s32[1024]{0:T(1024)S(1)} %pad_clamp_fusion), kind=kCustom, calls=%fused_computation | custom fusion | bytes 4194816 | tf_op jit(solution)/shard_map/jit(_take)/gather | solution.py:75
  23.7 2.5 gather.7
  26.7 0.3 select_select_fusion
  27.0 5.2 %copy.32 = bf16[1,512,2048]{2,0,1:T(2,128)(2,1)} copy(bf16[1,512,2048]{2,1,0:T(8,128)(2,1)S(1)} %select_select_fusion) | data formatting | bytes 4194304 | tf_op jit(solution)/shard_map/jit(_where)/select_n | solution.py:76
  32.2 0.5 broadcast.218
  32.7 13.1 %reduce.9 = bf16[512,2048]{1,0:T(8,128)(2,1)S(1)} reduce(bf16[512,1,2048]{2,1,0:T(2,128)(2,1)} %bitcast.34, bf16[]{:T(256)} %broadcast.218), dimensions={1}, to_apply=%bitcast.31.reduce_sub_computation | reduce | bytes 4194306
  45.8 2.8 reshape.240
  48.7 65.8 %all_to_all.10 = bf16[128,2,4096]{2,1,0:T(2,128)(2,1)S(1)} all-to-all(bf16[128,2,4096]{2,1,0:T(2,128)(2,1)} %reshape.240), channel_id=1, replica_groups=mesh['rep'=2,'shard'=128] {'shard'}, dimensions={0} | all-to-all | bytes 4194304 | tf_op jit(solution)/shard_map/all_to_all | solution.py:79
  114.4 6.8 %reshape.241 = bf16[512,1,2048]{2,1,0:T(2,128)(2,1)} reshape(bf16[128,2,4096]{2,1,0:T(2,128)(2,1)S(1)} %all_to_all.10) | data formatting | bytes 4194304
  121.2 4.8 %fusion.2 = f32[]{:T(128)} fusion(bf16[1,512,2048]{2,0,1:T(2,128)(2,1)} %bitcast.32), kind=kLoop, calls=%fused_computation.9 | loop fusion | flops 3145727 | bytes 2097156 | tf_op jit(solution)/shard_map/while/body/eval_jaxpr/reduce_sum | solution.py:18
  126.7 3.8 %fusion.5 = bf16[512,2048]{1,0:T(8,128)(2,1)S(1)} fusion(f32[]{:T(128)S(6)} %add.96, bf16[1,512,2048]{2,0,1:T(2,128)(2,1)} %bitcast.33), kind=kLoop, calls=%fused_computation.15 | loop fusion | flops 3145728 | bytes 4194308 | tf_op jit(solution)/shard_map/while/body/eval_jaxpr/convert_element_type | solution.py:19
  130.5 1.3 convolution_convert_fusion.2
  131.8 2.9 add_convert_fusion.1
  134.7 3.6 %convolution_convert_fusion.1 = bf16[512,512]{1,0:T(8,128)(2,1)S(1)} fusion(bf16[512,2048]{1,0:T(8,128)(2,1)} %add_convert_fusion.1), kind=kOutput, calls=%fused_computation.27 | convolution fusion | flops 1074003968 | bytes 2621440 | tf_op jit(solution)/shard_map/while/body/eval_jaxpr/dot_general | solution.py:22
  138.3 2.9 add_convert_fusion
  141.2 3.5 %convolution_convert_fusion = bf16[512,512]{1,0:T(8,128)(2,1)S(1)} fusion(bf16[512,2048]{1,0:T(8,128)(2,1)} %add_convert_fusion), kind=kOutput, calls=%fused_computation.26 | convolution fusion | flops 1074003968 | bytes 2621440 | tf_op jit(solution)/shard_map/while/body/eval_jaxpr/dot_general | solution.py:22
  144.7 3.8 %fusion.4 = bf16[1,512,2048]{2,1,0:T(8,128)(2,1)S(1)} fusion(bf16[512,2048]{1,0:T(8,128)(2,1)} %add_convert_fusion, bf16[512,512]{1,0:T(8,128)(2,1)S(1)} %convolution_convert_fusion), kind=kOutput, calls=%fused_computation.14 | convolution fusion | flops 1348730880 | bytes 4718592 | tf_op jit(solution)/shard_map/while/body/eval_jaxpr/dot_general | solution.py:27
  148.5 5.4 %copy.31 = bf16[1,512,2048]{2,0,1:T(2,128)(2,1)} copy(bf16[1,512,2048]{2,1,0:T(8,128)(2,1)S(1)} %fusion.4) | data formatting | bytes 4194304 | tf_op jit(solution)/shard_map/while/body/jit(dynamic_update_index_in_dim)/broadcast_in_dim | solution.py:78
  153.9 13.1 %reduce.10 = bf16[512,2048]{1,0:T(8,128)(2,1)S(1)} reduce(bf16[512,1,2048]{2,1,0:T(2,128)(2,1)} %bitcast.35, bf16[]{:T(256)} %broadcast.218), dimensions={1}, to_apply=%bitcast.30.reduce_sub_computation | reduce | bytes 4194306
  167.0 2.8 reshape.242
  169.9 58.7 %all_to_all.11 = bf16[128,2,4096]{2,1,0:T(2,128)(2,1)S(1)} all-to-all(bf16[128,2,4096]{2,1,0:T(2,128)(2,1)} %reshape.242), channel_id=1, replica_groups=mesh['rep'=2,'shard'=128] {'shard'}, dimensions={0} | all-to-all | bytes 4194304 | tf_op jit(solution)/shard_map/all_to_all | solution.py:81
  228.6 6.8 %reshape.243 = bf16[512,1,2048]{2,1,0:T(2,128)(2,1)} reshape(bf16[128,2,4096]{2,1,0:T(2,128)(2,1)S(1)} %all_to_all.11) | data formatting | bytes 4194304
  235.3 4.8 %copy.26 = bf16[1,512,2048]{2,1,0:T(8,128)(2,1)} copy(bf16[1,512,2048]{2,0,1:T(2,128)(2,1)} %bitcast.36) | data formatting | bytes 4194304 | tf_op jit(solution)/shard_map/all_to_all | solution.py:81
  240.2 17.8 %all-gather.2.cloned.1.call-done = bf16[2,512,2048]{2,1,0:T(8,128)(2,1)} async-done(((bf16[1,512,2048]{2,1,0:T(8,128)(2,1)}), bf16[2,512,2048]{2,1,0:T(8,128)(2,1)}) %all-gather.2.cloned.1.call-update) | async-done | bytes 4194320 | tf_op jit(solution)/shard_map/all_gather | solution.py:82
  258.0 7.2 %reshape.229 = bf16[256,4,2048]{2,1,0:T(4,128)(2,1)} reshape(bf16[2,512,2048]{2,1,0:T(8,128)(2,1)} %all-gather.2.cloned.1.call-done) | data formatting | bytes 8388608 | tf_op jit(solution)/shard_map/reshape | solution.py:54
  265.2 1.6 broadcast_in_dim.48
  266.8 22.2 %scatter_fusion = bf16[192,4,2048]{2,1,0:T(4,128)(2,1)S(1)} fusion(bf16[192,4,2048]{2,1,0:T(4,128)(2,1)S(1)} %broadcast_in_dim.48, s32[256]{0:T(256)S(1)} %bitcast.39, bf16[256,4,2048]{2,1,0:T(4,128)(2,1)} %reshape.229), kind=kCustom, calls=%fused_computation.2 | custom fusion | bytes 12583936 | tf_op jit(solution)/shard_map/scatter | solution.py:57
  289.0 1.7 copy-done
  (27 shorter events, 2.4 us)
Async XLA Ops:
  7.2 250.8 %all-gather.2.cloned.1.call-start = ((), (), s32[]{:S(2)}) async-start(), calls=%async_computation.2 | async-start | bytes 6291456 | tf_op jit(solution)/shard_map/all_gather | solution.py:82
  134.6 3.7 %copy-start.1 = (bf16[512,2048]{1,0:T(8,128)(2,1)S(1)}, bf16[512,2048]{1,0:T(8,128)(2,1)}, u32[]{:S(2)}) copy-start(bf16[512,2048]{1,0:T(8,128)(2,1)} %add_convert_fusion.1) | copy-start | bytes 6291460
  289.0 1.7 copy-start
Sparse Core Ops, SparseCore 0:
  240.3 17.6 all-gather.1
where the time goes:
time: 299 us; the launch traced here: 298 us
  blocking collectives  124 us (41%)
  local copies, waits for them, and re-layouts  78.6 us (26%)
  other arithmetic  43.7 us (15%)
  matrix products  18 us (6%)
  waiting for transfers between devices  17.8 us (6%)
  between operations  14.9 us (5%)
    all_to_all x1, blocking collectives, body(): lax.all_to_all(outgoing, 'shard', split_axis=1, concat_axis=1, tiled=True)  65.8 us
    all_to_all x1, blocking collectives, body(): lax.all_to_all(finished, 'shard', split_axis=1, concat_axis=1, tiled=True)  58.7 us
    unnamed x2, other arithmetic  26.2 us
    scatter x1, local copies, waits for them, and re-layouts, place_rows(): return empty.at[target].set(pieces, mode='drop')  22.2 us
    unnamed x10, local copies, waits for them, and re-layouts  22.2 us
    all_gather x1, waiting for transfers between devices, body(): both = lax.all_gather(returned, 'rep', axis=0, tiled=True)  17.8 us
    dot_general x3, matrix products, newton_schulz(): jnp.dot(mixer, current, preferred_element_type=jnp.float32)  9.57 us
    dot_general x3, matrix products, newton_schulz(): lax.dot_general(current, current, (((1,), (1,)), ((), ())), preferred_ele...  8.43 us
  transfers between devices with their start and end apart: 1, of which 1 were waited for; matrix products, arithmetic and copies ran while one was open for 0% of the time, Pallas kernels for 0%

commit v1 on v0

--- a/solution.py
+++ b/solution.py
@@ -79,7 +79,9 @@
         newton_schulz, lax.all_to_all(outgoing, "shard", split_axis=1, concat_axis=1, tiled=True)
     )
     returned = lax.all_to_all(finished, "shard", split_axis=1, concat_axis=1, tiled=True)
-    both = lax.all_gather(returned, "rep", axis=0, tiled=True)
+    both = jnp.concatenate(
+        lax.all_to_all(jnp.stack([returned] * lax.axis_size("rep")), "rep", 0, 0), axis=0
+    )
     every_choice = table.transpose(0, 2, 1).reshape(replicas * slot_count, shard_count)
     update = place_rows(both, every_choice, matrix_count)
     return (new_momentum, update)

time: 299 us -> 279 us (0.933)
  blocking collectives: 124 us -> 77.7 us
  waiting for transfers between devices: 17.8 us -> 49 us
  between operations: 14.9 us -> 1.54 us
  starting transfers between devices: 0.04 us -> 9.61 us
    all_to_all x0 -> x1, waiting for transfers between devices: none -> 49 us  [body(): lax.all_to_all(finished, 'shard', split_axis=1, concat_axis=1, tiled=True)]
    all_to_all x1, blocking collectives: 58.7 us -> 11.9 us  [body(): lax.all_to_all(jnp.stack([returned] * lax.axis_size('rep')), 'rep', 0, 0)]
    all_gather x1 -> x0, waiting for transfers between devices: 17.8 us -> none  [body(): both = lax.all_gather(returned, 'rep', axis=0, tiled=True)]
    all_to_all x0 -> x1, starting transfers between devices: none -> 9.61 us  [body(): lax.all_to_all(finished, 'shard', split_axis=1, concat_axis=1, tiled=True)]
    another operation x1 -> x2, local copies, waits for them, and re-layouts: 0.12 us -> 7.31 us  [the longest x1 7.19 us: place_rows(): returned.reshape(chosen.shape[0] * chosen.shape[1], local_rows, returned....]
    reshape x1 -> x0, local copies, waits for them, and re-layouts: 7.19 us -> none  [place_rows(): returned.reshape(chosen.shape[0] * chosen.shape[1], local_rows, returned....]
    all_to_all x1 -> x0, local copies, waits for them, and re-layouts: 4.78 us -> none  [body(): lax.all_to_all(finished, 'shard', split_axis=1, concat_axis=1, tiled=True)]
    unnamed x10 -> x11, local copies, waits for them, and re-layouts: 22.2 us -> 25.6 us
where the time goes in v1:
time: 279 us; the launch traced here: 277 us
  blocking collectives  77.7 us (28%)
  local copies, waits for them, and re-layouts  77.2 us (28%)
  waiting for transfers between devices  49 us (18%)
  other arithmetic  44.1 us (16%)
  matrix products  18 us (6%)
  starting transfers between devices  9.61 us (3%)
    all_to_all x1, blocking collectives, body(): lax.all_to_all(outgoing, 'shard', split_axis=1, concat_axis=1, tiled=True)  65.8 us
    all_to_all x1, waiting for transfers between devices, body(): lax.all_to_all(finished, 'shard', split_axis=1, concat_axis=1, tiled=True)  49 us
    unnamed x2, other arithmetic  26.2 us
    unnamed x11, local copies, waits for them, and re-layouts  25.6 us
    scatter x1, local copies, waits for them, and re-layouts, place_rows(): return empty.at[target].set(pieces, mode='drop')  22.2 us
    all_to_all x1, blocking collectives, body(): lax.all_to_all(jnp.stack([returned] * lax.axis_size('rep')), 'rep', 0, 0)  11.9 us
    all_to_all x1, starting transfers between devices, body(): lax.all_to_all(finished, 'shard', split_axis=1, concat_axis=1, tiled=True)  9.61 us
    dot_general x3, matrix products, newton_schulz(): jnp.dot(mixer, current, preferred_element_type=jnp.float32)  9.56 us
  transfers between devices with their start and end apart: 1, of which 1 were waited for; matrix products, arithmetic and copies ran while one was open for 0% of the time, Pallas kernels for 0%

profile of v1, /device:TPU:1, one launch (start us, length us, event | category | flops | bytes accessed | tf_op | source)
XLA Modules:
  0.0 277.2 jit_solution(11509632346757871590)
XLA Ops:
  0.6 0.7 fusion.27
  1.3 0.8 copy.20
  3.5 2.4 scatter_custom_fusion
  6.5 7.1 %fusion = (bf16[192,4,2048]{2,1,0:T(4,128)(2,1)S(1)}, bf16[192,4,2048]{2,1,0:T(4,128)(2,1)}) fusion(bf16[192,4,2048]{2,1,0:T(4,128)(2,1)} %param.3, bf16[192,4,2048]{2,1,0:T(4,128)(2,1)} %param.4), kind=kLoop, calls=%fused_computation.5 | loop fusion | flops 12582912 | bytes 12582912 | tf_op jit(solution)/shard_map/convert_element_type | solution.py:63
  13.6 3.5 %gather_fusion = bf16[128,4,2048]{2,1,0:T(4,128)(2,1)} fusion(bf16[192,4,2048]{2,1,0:T(4,128)(2,1)S(1)} %get-tuple-element.15, s32[1024]{0:T(1024)S(1)} %pad_clamp_fusion), kind=kCustom, calls=%fused_computation | custom fusion | bytes 4194816 | tf_op jit(solution)/shard_map/jit(_take)/gather | solution.py:75
  17.2 2.5 gather.7
  20.5 5.2 %copy.33 = bf16[1,512,2048]{2,0,1:T(2,128)(2,1)} copy(bf16[1,512,2048]{2,1,0:T(8,128)(2,1)S(1)} %select_select_fusion) | data formatting | bytes 4194304 | tf_op jit(solution)/shard_map/jit(_where)/select_n | solution.py:76
  25.6 0.5 broadcast.218
  26.1 13.1 %reduce.9 = bf16[512,2048]{1,0:T(8,128)(2,1)S(1)} reduce(bf16[512,1,2048]{2,1,0:T(2,128)(2,1)} %bitcast.39, bf16[]{:T(256)} %broadcast.218), dimensions={1}, to_apply=%bitcast.36.reduce_sub_computation | reduce | bytes 4194306
  39.3 2.8 %reshape.236 = bf16[128,2,4096]{2,1,0:T(2,128)(2,1)} reshape(bf16[512,2048]{1,0:T(8,128)(2,1)S(1)} %reduce.9) | data formatting | bytes 4194304
  42.1 65.8 %all_to_all.15 = bf16[128,2,4096]{2,1,0:T(2,128)(2,1)S(1)} all-to-all(bf16[128,2,4096]{2,1,0:T(2,128)(2,1)} %reshape.236), channel_id=1, replica_groups=mesh['rep'=2,'shard'=128] {'shard'}, dimensions={0} | all-to-all | bytes 4194304 | tf_op jit(solution)/shard_map/all_to_all | solution.py:79
  107.9 6.8 %reshape.237 = bf16[512,1,2048]{2,1,0:T(2,128)(2,1)} reshape(bf16[128,2,4096]{2,1,0:T(2,128)(2,1)S(1)} %all_to_all.15) | data formatting | bytes 4194304
  114.6 4.8 %fusion.2 = f32[]{:T(128)} fusion(bf16[1,512,2048]{2,0,1:T(2,128)(2,1)} %bitcast.37), kind=kLoop, calls=%fused_computation.9 | loop fusion | flops 3145727 | bytes 2097156 | tf_op jit(solution)/shard_map/while/body/eval_jaxpr/reduce_sum | solution.py:18
  120.1 3.8 %fusion.5 = bf16[512,2048]{1,0:T(8,128)(2,1)S(1)} fusion(f32[]{:T(128)S(6)} %add.96, bf16[1,512,2048]{2,0,1:T(2,128)(2,1)} %bitcast.38), kind=kLoop, calls=%fused_computation.16 | loop fusion | flops 3145728 | bytes 4194308 | tf_op jit(solution)/shard_map/while/body/eval_jaxpr/convert_element_type | solution.py:19
  123.9 1.3 convolution_convert_fusion.2
  125.2 2.9 %add_convert_fusion.1 = bf16[512,2048]{1,0:T(8,128)(2,1)} fusion(bf16[512,2048]{1,0:T(8,128)(2,1)S(1)} %fusion.5, bf16[512,512]{1,0:T(8,128)(2,1)S(1)} %convolution_convert_fusion.2), kind=kOutput, calls=%fused_computation.14 | convolution fusion | flops 1347682304 | bytes 4718592 | tf_op jit(solution)/shard_map/while/body/eval_jaxpr/dot_general | solution.py:27
  128.1 3.6 %convolution_convert_fusion.1 = bf16[512,512]{1,0:T(8,128)(2,1)S(1)} fusion(bf16[512,2048]{1,0:T(8,128)(2,1)} %add_convert_fusion.1), kind=kOutput, calls=%fused_computation.29 | convolution fusion | flops 1074003968 | bytes 2621440 | tf_op jit(solution)/shard_map/while/body/eval_jaxpr/dot_general | solution.py:22
  131.7 2.9 %add_convert_fusion = bf16[512,2048]{1,0:T(8,128)(2,1)} fusion(bf16[512,2048]{1,0:T(8,128)(2,1)S(1)} %copy-done.1, bf16[512,512]{1,0:T(8,128)(2,1)S(1)} %convolution_convert_fusion.1), kind=kOutput, calls=%fused_computation.13 | convolution fusion | flops 1347682304 | bytes 4718592 | tf_op jit(solution)/shard_map/while/body/eval_jaxpr/dot_general | solution.py:27
  134.6 3.5 %convolution_convert_fusion = bf16[512,512]{1,0:T(8,128)(2,1)S(1)} fusion(bf16[512,2048]{1,0:T(8,128)(2,1)} %add_convert_fusion), kind=kOutput, calls=%fused_computation.28 | convolution fusion | flops 1074003968 | bytes 2621440 | tf_op jit(solution)/shard_map/while/body/eval_jaxpr/dot_general | solution.py:22
  138.1 3.8 %fusion.4 = bf16[1,512,2048]{2,1,0:T(8,128)(2,1)S(1)} fusion(bf16[512,2048]{1,0:T(8,128)(2,1)} %add_convert_fusion, bf16[512,512]{1,0:T(8,128)(2,1)S(1)} %convolution_convert_fusion), kind=kOutput, calls=%fused_computation.15 | convolution fusion | flops 1348730880 | bytes 4718592 | tf_op jit(solution)/shard_map/while/body/eval_jaxpr/dot_general | solution.py:27
  141.9 5.4 %copy.32 = bf16[1,512,2048]{2,0,1:T(2,128)(2,1)} copy(bf16[1,512,2048]{2,1,0:T(8,128)(2,1)S(1)} %fusion.4) | data formatting | bytes 4194304 | tf_op jit(solution)/shard_map/while/body/jit(dynamic_update_index_in_dim)/broadcast_in_dim | solution.py:78
  147.3 13.1 %reduce.10 = bf16[512,2048]{1,0:T(8,128)(2,1)S(1)} reduce(bf16[512,1,2048]{2,1,0:T(2,128)(2,1)} %bitcast.40, bf16[]{:T(256)} %broadcast.218), dimensions={1}, to_apply=%bitcast.35.reduce_sub_computation | reduce | bytes 4194306
  160.4 2.8 %reshape.238 = bf16[128,2,4096]{2,1,0:T(2,128)(2,1)} reshape(bf16[512,2048]{1,0:T(8,128)(2,1)S(1)} %reduce.10) | data formatting | bytes 4194304
  163.3 9.6 %all-to-all-start.1 = ((bf16[128,2,4096]{2,1,0:T(2,128)(2,1)}), bf16[128,2,4096]{2,1,0:T(2,128)(2,1)S(1)}, u32[]{:S(2)}, u32[]{:S(2)}) async-start(bf16[128,2,4096]{2,1,0:T(2,128)(2,1)} %reshape.238), calls=%async_computation.1 | async-start | bytes 4194304 | tf_op jit(solution)/shard_map/all_to_all | solution.py:81
  172.9 49.0 %all-to-all-done.1 = bf16[128,2,4096]{2,1,0:T(2,128)(2,1)S(1)} async-done(((bf16[128,2,4096]{2,1,0:T(2,128)(2,1)}), bf16[128,2,4096]{2,1,0:T(2,128)(2,1)S(1)}, u32[]{:S(2)}, u32[]{:S(2)}) %all-to-all-start.1) | async-done | bytes 2097184 | tf_op jit(solution)/shard_map/all_to_all | solution.py:81
  222.0 6.8 %reshape.239 = bf16[512,1,2048]{2,1,0:T(2,128)(2,1)} reshape(bf16[128,2,4096]{2,1,0:T(2,128)(2,1)S(1)} %all-to-all-done.1) | data formatting | bytes 4194304
  228.8 3.5 %copy.31 = bf16[1,512,2048]{2,1,0:T(8,128)(2,1)S(1)} copy(bf16[1,512,2048]{2,0,1:T(2,128)(2,1)} %bitcast.41) | data formatting | bytes 4194304
  232.6 11.9 %all_to_all.16 = bf16[2,1,512,2048]{3,2,1,0:T(8,128)(2,1)} all-to-all(bf16[2,1,512,2048]{3,2,1,0:T(8,128)(2,1)S(1)} %pad_maximum_fusion), channel_id=1, replica_groups=mesh['rep'=2,'shard'=128] {'rep'}, dimensions={0} | all-to-all | bytes 8388608 | tf_op jit(solution)/shard_map/all_to_all | solution.py:83
  244.5 7.2 %reshape.225 = bf16[256,4,2048]{2,1,0:T(4,128)(2,1)} reshape(bf16[2,1,512,2048]{3,2,1,0:T(8,128)(2,1)} %all_to_all.16) | data formatting | bytes 8388608 | tf_op jit(solution)/shard_map/reshape;reshape | solution.py:54
  251.7 1.6 broadcast_in_dim.48
  253.3 22.2 %scatter_fusion = bf16[192,4,2048]{2,1,0:T(4,128)(2,1)S(1)} fusion(bf16[192,4,2048]{2,1,0:T(4,128)(2,1)S(1)} %broadcast_in_dim.48, s32[256]{0:T(256)S(1)} %bitcast.45, bf16[256,4,2048]{2,1,0:T(4,128)(2,1)} %reshape.225), kind=kCustom, calls=%fused_computation.2 | custom fusion | bytes 12583936 | tf_op jit(solution)/shard_map/scatter | solution.py:57
  275.6 1.7 copy-done
  (27 shorter events, 3.1 us)
Async XLA Ops:
  128.1 3.7 %copy-start.1 = (bf16[512,2048]{1,0:T(8,128)(2,1)S(1)}, bf16[512,2048]{1,0:T(8,128)(2,1)}, u32[]{:S(2)}) copy-start(bf16[512,2048]{1,0:T(8,128)(2,1)} %add_convert_fusion.1) | copy-start | bytes 6291460
  163.3 58.7 %all-to-all-start.1 = ((bf16[128,2,4096]{2,1,0:T(2,128)(2,1)}), bf16[128,2,4096]{2,1,0:T(2,128)(2,1)S(1)}, u32[]{:S(2)}, u32[]{:S(2)}) async-start(bf16[128,2,4096]{2,1,0:T(2,128)(2,1)} %reshape.238), calls=%async_computation.1 | async-start | bytes 4194304 | tf_op jit(solution)/shard_map/all_to_all | solution.py:81
  275.6 1.7 copy-start
